TPU v7x, 32 devices: a whole 2x2x4 slice. The times are simulated.
32 devices in a mesh: depth: 8 (over y, x, core), row: 4 (over z).
Axes of the slice: x: 2, y: 2, z: 4, core: 2. Of those that a mesh axis runs over, the one named last changes fastest.
Arguments:
- input_cells: bfloat16 [32, 64, 128, 128], P('depth', 'row'), may hold values from -6 to 6
- first_weight: bfloat16 [3, 3, 3, 64, 128], P(None, None, None, None, 'depth'), may hold values from -0.15625 to 0.15625
- second_weight: bfloat16 [3, 3, 3, 128, 256], P(None, None, None, None, 'depth'), may hold values from -0.109375 to 0.109375
Outputs:
- encoded: bfloat16 [8, 16, 32, 512], P('depth', 'row')
All inputs are finite; a program needn't handle non-finite values.
Results may differ from a plain program's by a relative error of at most 0.0049.
Values may be sent and summed in bfloat16 or wider, within the bound.
A program may use at most 64 MiB of HBM per device.

v0:
```python
import jax
import jax.numpy as jnp
from jax import lax
from jax.sharding import PartitionSpec as P


def from_behind(x, axis, by):
    count = lax.axis_size(axis)
    pairs = [(i, i + by) for i in range(count) if 0 <= i + by < count]
    return lax.ppermute(x, axis, pairs)


def stacked(weight, depth_tap, row_tap):
    kernel_taps = weight[depth_tap, row_tap]
    zeros_block = jnp.zeros_like(kernel_taps[0])
    upper_part = jnp.concatenate([kernel_taps[1], kernel_taps[2]], 0)
    lower_part = jnp.concatenate([zeros_block, kernel_taps[0]], 0)
    return jnp.concatenate([upper_part, lower_part], 1)


def convolve(extended, weight):
    planes = extended.shape[0] - 1
    row_count = extended.shape[1] - 1
    pair_count = extended.shape[2]
    features = extended.shape[3]
    out_width = weight.shape[4]
    running = jnp.zeros((planes // 2 * (row_count // 2) * pair_count, 2 * out_width), jnp.float32)
    for depth_tap in range(3):
        for row_tap in range(3):
            window = extended[depth_tap : depth_tap + planes : 2, row_tap : row_tap + row_count : 2]
            running = running + jnp.dot(
                window.reshape(-1, features),
                stacked(weight, depth_tap, row_tap),
                preferred_element_type=jnp.float32,
            )
    running = running.reshape(planes // 2, row_count // 2, pair_count, 2 * out_width)
    carried = jnp.pad(running[:, :, :-1, out_width:], ((0, 0), (0, 0), (1, 0), (0, 0)))
    return running[..., :out_width] + carried


def finish(field):
    activated = jnp.maximum(field, 0.0).astype(jnp.bfloat16)
    shape_now = activated.shape
    return activated.reshape(shape_now[0], shape_now[1], shape_now[2] // 2, 2 * shape_now[3])


def per_device(input_cells, first_weight, second_weight):
    first_full, second_full = (
        lax.all_gather(first_weight, "depth", axis=4, tiled=True),
        lax.all_gather(second_weight, "depth", axis=4, tiled=True),
    )
    below_plane = from_behind(input_cells[-1:], "depth", 1)
    with_plane = jnp.concatenate([below_plane, input_cells], 0)
    below_row = from_behind(with_plane[:, -1:], "row", 1)
    extended = jnp.concatenate([below_row, with_plane], 1)
    hidden = finish(convolve(extended, first_full))
    hidden_below = from_behind(hidden[-1:], "depth", 1)
    hidden_plus = jnp.concatenate([hidden_below, hidden], 0)
    hidden_rowrim = from_behind(hidden_plus[:, -1:], "row", 1)
    hidden_ext = jnp.concatenate([hidden_rowrim, hidden_plus], 1)
    summed = convolve(hidden_ext, second_full)
    return finish(summed)


def solution(mesh):
    return jax.shard_map(
        per_device,
        mesh=mesh,
        in_specs=(
            P("depth", "row", None, None),
            P(None, None, None, None, "depth"),
            P(None, None, None, None, "depth"),
        ),
        out_specs=P("depth", "row", None, None),
        check_vma=False,
    )
```

profile of v0, /device:TPU:29, one launch (start us, length us, event | category | flops | bytes accessed | tf_op | source)
XLA Modules:
  0.0 71.3 jit_solution(71455804238040424)
XLA Ops:
  6.5 0.7 all-gather.2.cloned.1.call-update
  7.3 1.1 %slice.378 = bf16[1,16,128,128]{3,2,1,0:T(8,128)(2,1)S(1)} slice(bf16[4,16,128,128]{3,2,1,0:T(8,128)(2,1)} %param.3), slice={[3:4], [0:16], [0:128], [0:128]} | slice | bytes 1048576 | tf_op jit(solution)/shard_map/slice | solution.py:52
  8.4 3.8 %collective-permute-start = (bf16[1,16,128,128]{3,2,1,0:T(8,128)(2,1)S(1)}, bf16[1,16,128,128]{3,2,1,0:T(8,128)(2,1)S(1)}, u32[]{:S(2)}, u32[]{:S(2)}) collective-permute-start(bf16[1,16,128,128]{3,2,1,0:T(8,128)(2,1)S(1)} %slice.378), channel_id=1, source_target_pairs={{0,4},{4,8},{8,12},{12,16},{16,20},{20,24},{24,28},{1,5},{5,9},{9,... | collective-permute-start | bytes 1572872 | tf_op jit(solution)/shard_map/ppermute | solution.py:10
  12.2 1.7 %fusion.230 = (bf16[2,8,128,128]{3,2,1,0:T(8,128)(2,1)S(1)}, bf16[2,8,128,128]{3,2,1,0:T(8,128)(2,1)S(1)}, bf16[2,8,128,128]{3,2,1,0:T(8,128)(2,1)S(1)}, bf16[2,8,128,128]{3,2,1,0:T(8,128)(2,1)S(1)}) fusion(bf16[4,16,128,128]{3,2,1,0:T(8,128)(2,1)} %param.3), kind=kLoop, calls=%fused_computation.291 | loop fusion | bytes 4194304 | tf_op jit(solution)/shard_map/slice | solution.py:30
  13.9 16.0 %all_gather.6 = bf16[3,3,3,64,128]{3,4,2,1,0:T(8,128)(2,1)S(1)} all-gather(bf16[3,3,3,64,16]{3,4,2,1,0:T(8,128)(2,1)S(1)} %copy-done.2), channel_id=1, replica_groups=mesh['depth'=8,'row'=4] {'depth'}, dimensions={4}, use_global_device_ids=true | all-gather | bytes 497664 | tf_op jit(solution)/shard_map/all_gather | solution.py:49
  30.0 0.5 convolution_bitcast_fusion.3
  30.5 0.5 convolution_bitcast_fusion.1
  31.1 1.1 %copy-done = bf16[4,16,128,128]{3,2,1,0:T(8,128)(2,1)S(1)} copy-done((bf16[4,16,128,128]{3,2,1,0:T(8,128)(2,1)S(1)}, bf16[4,16,128,128]{3,2,1,0:T(8,128)(2,1)}, u32[]{:S(2)}) %copy-start) | copy-done | bytes 2097176
  32.2 0.3 constant_dynamic-update-slice_fusion
  32.6 1.3 %collective-permute-start.1 = (bf16[5,1,128,128]{3,2,1,0:T(8,128)(2,1)S(1)}, bf16[5,1,128,128]{3,2,1,0:T(8,128)(2,1)S(1)}, u32[]{:S(2)}, u32[]{:S(2)}) collective-permute-start(bf16[5,1,128,128]{3,2,1,0:T(8,128)(2,1)S(1)} %slice.459), channel_id=1, source_target_pairs={{0,1},{1,2},{2,3},{4,5},{5,6},{6,7},{8,9},{9,10},{10,11},{12,13},{... | collective-permute-start | bytes 491528 | tf_op jit(solution)/shard_map/ppermute | solution.py:10
  33.9 0.5 fusion.106
  34.4 0.5 fusion.103
  34.9 4.7 %collective-permute-done.1 = bf16[5,1,128,128]{3,2,1,0:T(8,128)(2,1)S(1)} collective-permute-done((bf16[5,1,128,128]{3,2,1,0:T(8,128)(2,1)S(1)}, bf16[5,1,128,128]{3,2,1,0:T(8,128)(2,1)S(1)}, u32[]{:S(2)}, u32[]{:S(2)}) %collective-permute-start.1) | collective-permute-done | bytes 163872 | tf_op jit(solution)/shard_map/ppermute | solution.py:10
  40.0 0.5 fusion.4
  40.5 0.5 fusion.3
  41.0 0.5 fusion
  41.5 0.6 fusion.2
  42.2 0.5 fusion.1
  43.1 6.9 %collective-permute-start.2 = (bf16[1,8,64,256]{3,2,1,0:T(8,128)(2,1)S(1)}, bf16[1,8,64,256]{3,2,1,0:T(8,128)(2,1)S(1)}, u32[]{:S(2)}, u32[]{:S(2)}) collective-permute-start(bf16[1,8,64,256]{3,2,1,0:T(8,128)(2,1)S(1)} %slice.419), channel_id=1, source_target_pairs={{0,4},{4,8},{8,12},{12,16},{16,20},{20,24},{24,28},{1,5},{5,9},{9,... | collective-permute-start | bytes 786440 | tf_op jit(solution)/shard_map/ppermute | solution.py:10
  50.2 3.1 %collective-permute-done.2 = bf16[1,8,64,256]{3,2,1,0:T(8,128)(2,1)S(1)} collective-permute-done((bf16[1,8,64,256]{3,2,1,0:T(8,128)(2,1)S(1)}, bf16[1,8,64,256]{3,2,1,0:T(8,128)(2,1)S(1)}, u32[]{:S(2)}, u32[]{:S(2)}) %collective-permute-start.2) | collective-permute-done | bytes 262176 | tf_op jit(solution)/shard_map/ppermute | solution.py:10
  53.4 1.3 %collective-permute-start.3 = (bf16[3,1,64,256]{3,2,1,0:T(8,128)(2,1)S(1)}, bf16[3,1,64,256]{3,2,1,0:T(8,128)(2,1)S(1)}, u32[]{:S(2)}, u32[]{:S(2)}) collective-permute-start(bf16[3,1,64,256]{3,2,1,0:T(8,128)(2,1)S(1)} %slice.490), channel_id=1, source_target_pairs={{0,1},{1,2},{2,3},{4,5},{5,6},{6,7},{8,9},{9,10},{10,11},{12,13},{... | collective-permute-start | bytes 294920 | tf_op jit(solution)/shard_map/ppermute | solution.py:10
  54.7 5.0 %collective-permute-done.3 = bf16[3,1,64,256]{3,2,1,0:T(8,128)(2,1)S(1)} collective-permute-done((bf16[3,1,64,256]{3,2,1,0:T(8,128)(2,1)S(1)}, bf16[3,1,64,256]{3,2,1,0:T(8,128)(2,1)S(1)}, u32[]{:S(2)}, u32[]{:S(2)}) %collective-permute-start.3) | collective-permute-done | bytes 98336 | tf_op jit(solution)/shard_map/ppermute | solution.py:10
  59.9 1.2 %slice_bitcast_fusion.20 = (bf16[128,256]{0,1:T(8,128)(2,1)S(1)}, bf16[128,256]{0,1:T(8,128)(2,1)S(1)}, bf16[128,256]{0,1:T(8,128)(2,1)S(1)}, bf16[128,256]{0,1:...) fusion(bf16[3,3,3,128,256]{3,4,2,1,0:T(8,128)(2,1)} %all-gather, ...), kind=kLoop, calls=%fused_computation.143 | loop fusion | bytes 1048576 | tf_op jit(solution)/shard_map/squeeze | solution.py:16
  61.4 0.3 convolution_add_fusion.10
  61.8 0.3 convolution_add_fusion.9
  62.0 0.3 convolution_add_fusion.8
  62.3 0.3 convolution_add_fusion.7
  62.6 0.3 convolution_add_fusion.6
  62.8 0.3 convolution_add_fusion.5
  63.1 0.3 convolution_add_fusion.4
  63.4 0.3 convolution_add_fusion.3
  63.7 0.7 reshape.196
  (31 shorter events, 1.9 us)
Async XLA Ops:
  6.5 53.3 %all-gather.2.cloned.1.call-start = ((), (), s32[]{:S(2)}) async-start(), calls=%async_computation | async-start | bytes 1990656 | tf_op jit(solution)/shard_map/all_gather | solution.py:50
  8.3 5.5 %copy-start.2 = (bf16[3,3,3,64,16]{3,4,2,1,0:T(8,128)(2,1)S(1)}, bf16[3,3,3,64,16]{3,4,2,1,0:T(8,128)(2,1)}, u32[]{:S(2)}) copy-start(bf16[3,3,3,64,16]{3,4,2,1,0:T(8,128)(2,1)} %param.4) | copy-start | bytes 165892
  8.4 22.7 %collective-permute-start = (bf16[1,16,128,128]{3,2,1,0:T(8,128)(2,1)S(1)}, bf16[1,16,128,128]{3,2,1,0:T(8,128)(2,1)S(1)}, u32[]{:S(2)}, u32[]{:S(2)}) collective-permute-start(bf16[1,16,128,128]{3,2,1,0:T(8,128)(2,1)S(1)} %slice.378), channel_id=1, source_target_pairs={{0,4},{4,8},{8,12},{12,16},{16,20},{20,24},{24,28},{1,5},{5,9},{9,... | collective-permute-start | bytes 1572872 | tf_op jit(solution)/shard_map/ppermute | solution.py:10
  30.5 1.7 %copy-start = (bf16[4,16,128,128]{3,2,1,0:T(8,128)(2,1)S(1)}, bf16[4,16,128,128]{3,2,1,0:T(8,128)(2,1)}, u32[]{:S(2)}) copy-start(bf16[4,16,128,128]{3,2,1,0:T(8,128)(2,1)} %param.3) | copy-start | bytes 6291460
  32.6 7.0 %collective-permute-start.1 = (bf16[5,1,128,128]{3,2,1,0:T(8,128)(2,1)S(1)}, bf16[5,1,128,128]{3,2,1,0:T(8,128)(2,1)S(1)}, u32[]{:S(2)}, u32[]{:S(2)}) collective-permute-start(bf16[5,1,128,128]{3,2,1,0:T(8,128)(2,1)S(1)} %slice.459), channel_id=1, source_target_pairs={{0,1},{1,2},{2,3},{4,5},{5,6},{6,7},{8,9},{9,10},{10,11},{12,13},{... | collective-permute-start | bytes 491528 | tf_op jit(solution)/shard_map/ppermute | solution.py:10
  43.1 10.2 %collective-permute-start.2 = (bf16[1,8,64,256]{3,2,1,0:T(8,128)(2,1)S(1)}, bf16[1,8,64,256]{3,2,1,0:T(8,128)(2,1)S(1)}, u32[]{:S(2)}, u32[]{:S(2)}) collective-permute-start(bf16[1,8,64,256]{3,2,1,0:T(8,128)(2,1)S(1)} %slice.419), channel_id=1, source_target_pairs={{0,4},{4,8},{8,12},{12,16},{16,20},{20,24},{24,28},{1,5},{5,9},{9,... | collective-permute-start | bytes 786440 | tf_op jit(solution)/shard_map/ppermute | solution.py:10
  53.4 6.3 %collective-permute-start.3 = (bf16[3,1,64,256]{3,2,1,0:T(8,128)(2,1)S(1)}, bf16[3,1,64,256]{3,2,1,0:T(8,128)(2,1)S(1)}, u32[]{:S(2)}, u32[]{:S(2)}) collective-permute-start(bf16[3,1,64,256]{3,2,1,0:T(8,128)(2,1)S(1)} %slice.490), channel_id=1, source_target_pairs={{0,1},{1,2},{2,3},{4,5},{5,6},{6,7},{8,9},{9,10},{10,11},{12,13},{... | collective-permute-start | bytes 294920 | tf_op jit(solution)/shard_map/ppermute | solution.py:10
  59.9 1.8 %copy-start.1 = (bf16[3,3,3,128,256]{3,4,2,1,0:T(8,128)(2,1)S(1)}, bf16[3,3,3,128,256]{3,4,2,1,0:T(8,128)(2,1)}, u32[]{:S(2)}) copy-start(bf16[3,3,3,128,256]{3,4,2,1,0:T(8,128)(2,1)} %all-gather.2.cloned.1.call-done) | copy-start | bytes 5308420
Sparse Core Ops, SparseCore 0:
  9.2 29.6 all-gather.1
where the time goes:
time: 72.5 us; the launch traced here: 71.3 us
  blocking collectives  16 us (22%)
  between operations  13.8 us (19%)
  waiting for transfers between devices  13.5 us (19%)
  starting transfers between devices  13.3 us (18%)
  local copies, waits for them, and re-layouts  7.11 us (10%)
  matrix products  7.06 us (10%)
    all_gather x1, blocking collectives, per_device(): lax.all_gather(first_weight, 'depth', axis=4, tiled=True)  16 us
    ppermute x4, starting transfers between devices, from_behind(): return lax.ppermute(x, axis, pairs)  13.3 us
    ppermute x4, waiting for transfers between devices, from_behind(): return lax.ppermute(x, axis, pairs)  12.7 us
    dot_general x18, matrix products, convolve(): jnp.dot(window.reshape(-1, features), stacked(weight, depth_tap, row_tap)...  7.06 us
    slice x6, local copies, waits for them, and re-layouts, convolve(): extended[depth_tap:depth_tap + planes:2, row_tap:row_tap + row_count:2]  2.07 us
  transfers between devices with their start and end apart: 5, of which 3 were waited for; matrix products, arithmetic and copies ran while one was open for 13% of the time, Pallas kernels for 0%

commit v1 on v0

v1 whole, which is shorter than its diff:
```python
import functools

import jax
import jax.numpy as jnp
from jax import lax
from jax.experimental import pallas as pl
from jax.experimental.pallas import tpu as pltpu
from jax.sharding import PartitionSpec as P

MESH = pl.DeviceIdType.MESH
BF16, F32 = jnp.bfloat16, jnp.float32


def dot_nt(lhs, rhs):
    return lax.dot_general(lhs, rhs, (((1,), (1,)), ((), ())), preferred_element_type=F32)


def merged(block):
    n, ch, k = block.shape
    if ch % 16 == 0:
        return block.reshape(n * ch, k)
    return jnp.concatenate([block[s].astype(F32) for s in range(n)], 0).astype(BF16)


def shift_pairs(low, pairs):
    rolled = pltpu.roll(low, 1, 0)
    at = lax.broadcasted_iota(jnp.int32, low.shape, 0)
    return jnp.where(lax.rem(at, pairs) == 0, 0.0, rolled)


def kernel(n, rows_n, x_ref, w1_ref, w2_ref, o_ref, ext, g1, g2, hid, tmp, tmp2,
           x_sem, own_sem, h_send, h_recv, w1_send, w1_fwd, w1_recv,
           w2_send, w2_fwd, w2_recv, hh_send, hh_recv):
    d, r = lax.axis_index("depth"), lax.axis_index("row")
    planes, qs = x_ref.shape[0], x_ref.shape[1]
    pairs, feats = x_ref.shape[3], x_ref.shape[4]
    c1 = feats // 2
    mid = n * w1_ref.shape[1]
    out_ch = n * w2_ref.shape[1]
    hplanes, hrows = planes // 2, qs
    hq = hrows // 2
    hpairs = pairs // 2

    has_next_d, has_prev_d = d < n - 1, d > 0
    has_next_r, has_prev_r = r < rows_n - 1, r > 0
    parity = lax.rem(d, 2)
    partner = d + 1 - 2 * parity

    own_x = [
        pltpu.make_async_copy(x_ref.at[:, :, 0], ext.at[1:planes + 1, 0:qs, 1], x_sem.at[0]),
        pltpu.make_async_copy(x_ref.at[:, :, 1], ext.at[1:planes + 1, 1:qs + 1, 0], x_sem.at[1]),
    ]
    for c in own_x:
        c.start()
    own_w2 = pltpu.make_async_copy(w2_ref, g2.at[:, d], own_sem.at[0])
    own_w2.start()

    barrier = pltpu.get_barrier_semaphore()
    for k in range(1, n):
        pl.semaphore_signal(barrier, inc=1, device_id=(lax.rem(d + k, n), r), device_id_type=MESH)

    @pl.when(has_next_r)
    def _():
        pl.semaphore_signal(barrier, inc=1, device_id=(d, r + 1), device_id_type=MESH)

    @pl.when(has_prev_r)
    def _():
        pl.semaphore_signal(barrier, inc=1, device_id=(d, r - 1), device_id_type=MESH)

    @pl.when(has_next_r & has_next_d)
    def _():
        pl.semaphore_signal(barrier, inc=1, device_id=(d + 1, r + 1), device_id_type=MESH)

    @pl.when(has_prev_r & has_prev_d)
    def _():
        pl.semaphore_signal(barrier, inc=1, device_id=(d - 1, r - 1), device_id_type=MESH)

    zero_half = jnp.zeros((w1_ref.shape[1], c1), BF16)
    for ij in range(9):
        g1[ij, d] = jnp.concatenate([w1_ref[3 * ij + 1], w1_ref[3 * ij + 2]], 1)
        g1[9 + ij, d] = jnp.concatenate([zero_half, w1_ref[3 * ij]], 1)

    @pl.when(jnp.logical_not(has_prev_d))
    def _():
        ext[0] = jnp.zeros(ext.shape[1:], BF16)
        hid[0] = jnp.zeros(hid.shape[1:], BF16)

    @pl.when(jnp.logical_not(has_prev_r))
    def _():
        ext[:, 0, 0] = jnp.zeros((planes + 1, pairs, feats), BF16)
        hid[:, 0, 0] = jnp.zeros((hplanes + 1, hpairs, 2 * mid), BF16)

    expected = (n - 1 + has_next_r.astype(jnp.int32) + has_prev_r.astype(jnp.int32)
                + (has_next_r & has_next_d).astype(jnp.int32)
                + (has_prev_r & has_prev_d).astype(jnp.int32))
    pl.semaphore_wait(barrier, expected)

    def remote(src, dst, ssem, rsem, to):
        return pltpu.make_async_remote_copy(
            src_ref=src, dst_ref=dst, send_sem=ssem, recv_sem=rsem,
            device_id=to, device_id_type=MESH)

    def weight_copy(src, buf, owner, ssem, rsem, to):
        return remote(src, buf.at[:, owner], ssem, rsem.at[owner], (to, r))

    def same(k):
        return lax.rem(d + 2 * k, n)

    w1_out = [weight_copy(g1.at[:, d], g1, d, w1_send.at[0], w1_recv, partner)]
    w2_out = [weight_copy(w2_ref, g2, d, w2_send.at[0], w2_recv, partner)]
    for k in range(1, n // 2):
        w1_out.append(weight_copy(g1.at[:, d], g1, d, w1_send.at[k], w1_recv, same(k)))
        w2_out.append(weight_copy(w2_ref, g2, d, w2_send.at[k], w2_recv, same(k)))
    w1_on = [weight_copy(g1.at[:, same(k)], g1, same(k), w1_fwd.at[k], w1_recv, partner) for k in range(1, n // 2)]
    w2_on = [weight_copy(g2.at[:, same(k)], g2, same(k), w2_fwd.at[k], w2_recv, partner) for k in range(1, n // 2)]

    def arrived(buf, rsem, owner):
        remote(buf.at[:, owner], buf.at[:, owner], rsem.at[owner], rsem.at[owner], (partner, r)).wait_recv()

    next_d, next_r = lax.rem(d + 1, n), lax.rem(r + 1, rows_n)
    plane_out = [
        remote(x_ref.at[planes - 1, :, 0], ext.at[0, 0:qs, 1], h_send.at[0], h_recv.at[0], (next_d, r)),
        remote(x_ref.at[planes - 1, :, 1], ext.at[0, 1:qs + 1, 0], h_send.at[1], h_recv.at[1], (next_d, r)),
    ]
    row_out = [remote(x_ref.at[:, qs - 1, 1], ext.at[1:planes + 1, 0, 0], h_send.at[2], h_recv.at[2], (d, next_r))]
    corner_out = [remote(x_ref.at[planes - 1, qs - 1, 1], ext.at[0, 0, 0], h_send.at[3], h_recv.at[3], (next_d, next_r))]

    def when_start(cond, copies):
        @pl.when(cond)
        def _():
            for c in copies:
                c.start()

    def when_recv(cond, copies):
        @pl.when(cond)
        def _():
            for c in copies:
                c.wait_recv()

    def when_sent(cond, copies):
        @pl.when(cond)
        def _():
            for c in copies:
                c.wait_send()

    for c in w1_out:
        c.start()
    when_start(has_next_r, row_out)
    when_start(has_next_d, plane_out)
    when_start(has_next_d & has_next_r, corner_out)
    for c in w2_out:
        c.start()

    for k in range(1, n // 2):
        arrived(g1, w1_recv, same(k))
        w1_on[k - 1].start()
    for k in range(0, n // 2):
        arrived(g1, w1_recv, lax.rem(partner + 2 * k, n))
    for c in own_x:
        c.wait()
    when_recv(has_prev_r, row_out)

    rhs1 = jnp.concatenate(
        [jnp.concatenate([merged(g1[ij]), merged(g1[9 + ij])], 0) for ij in range(9)], 1)

    def first(a):
        wins = []
        for i in range(3):
            for j in range(3):
                w = ext[2 * a + i, j // 2:j // 2 + qs, j % 2]
                wins.append(w.reshape(qs * pairs, feats))
        res = dot_nt(jnp.concatenate(wins, 1), rhs1)
        val = jnp.maximum(res[:, :mid] + shift_pairs(res[:, mid:], pairs), 0.0)
        tmp[...] = val
        half = qs * hpairs
        for s in range(2):
            part = tmp[pl.ds(s, half, 2), :].astype(BF16).reshape(hq, 2, hpairs, mid)
            hid[a + 1, 0:hq, 1, :, s * mid:(s + 1) * mid] = part[:, 0]
            hid[a + 1, 1:hq + 1, 0, :, s * mid:(s + 1) * mid] = part[:, 1]

    last = hplanes
    hplane_out = [
        remote(hid.at[last, 0:hq, 1], hid.at[0, 0:hq, 1], hh_send.at[0], hh_recv.at[0], (next_d, r)),
        remote(hid.at[last, 1:hq + 1, 0], hid.at[0, 1:hq + 1, 0], hh_send.at[1], hh_recv.at[1], (next_d, r)),
    ]
    hcorner_out = [remote(hid.at[last, hq, 0], hid.at[0, 0, 0], hh_send.at[2], hh_recv.at[2], (next_d, next_r))]
    hrow_out = [remote(hid.at[a + 1, hq, 0], hid.at[a + 1, 0, 0], hh_send.at[3 + a], hh_recv.at[3 + a], (d, next_r))
                for a in range(hplanes)]

    for a in range(hplanes - 1, -1, -1):
        if a == 0:
            when_recv(has_prev_d, plane_out)
            when_recv(has_prev_d & has_prev_r, corner_out)
        first(a)
        if a == hplanes - 1:
            when_start(has_next_d, hplane_out)
            when_start(has_next_d & has_next_r, hcorner_out)
        when_start(has_next_r, [hrow_out[a]])

    for k in range(1, n // 2):
        arrived(g2, w2_recv, same(k))
        w2_on[k - 1].start()
    for k in range(0, n // 2):
        arrived(g2, w2_recv, lax.rem(partner + 2 * k, n))
    own_w2.wait()
    when_recv(has_prev_r, hrow_out)
    when_recv(has_prev_d, hplane_out)
    when_recv(has_prev_d & has_prev_r, hcorner_out)

    for a in range(hplanes // 2):
        wins, rights, ups, lows = [], [], [], []
        for i in range(3):
            for j in range(3):
                w = hid[2 * a + i, j // 2:j // 2 + hq, j % 2].reshape(hq * hpairs, 2 * mid)
                wins.append(w)
                rights.append(w[:, mid:])
                t = 3 * (3 * i + j)
                ups += [merged(g2[t + 1]), merged(g2[t + 2])]
                lows.append(merged(g2[t]))
        up = dot_nt(jnp.concatenate(wins, 1), jnp.concatenate(ups, 1))
        low = dot_nt(jnp.concatenate(rights, 1), jnp.concatenate(lows, 1))
        val = jnp.maximum(up + shift_pairs(low, hpairs), 0.0)
        half = hq * hpairs // 2
        for h in range(out_ch // 128):
            tmp2[h] = val[:, h * 128:(h + 1) * 128]
        for s in range(2):
            for h in range(out_ch // 128):
                part = tmp2[h, pl.ds(s, half, 2), :].astype(BF16).reshape(hq, hpairs // 2, 128)
                at = s * out_ch + h * 128
                o_ref[a, :, :, at:at + 128] = part

    for c in w1_out + w1_on + w2_out + w2_on:
        c.wait_send()
    when_sent(has_next_r, row_out + hrow_out)
    when_sent(has_next_d, plane_out + hplane_out)
    when_sent(has_next_d & has_next_r, corner_out + hcorner_out)


def solution(mesh):
    n, rows_n = mesh.shape["depth"], mesh.shape["row"]

    def per_device(x, w1, w2):
        planes, rows, pairs, feats = x.shape
        ch1, ch2 = w1.shape[4], w2.shape[4]
        mid, out_ch = n * ch1, n * ch2
        qs = rows // 2
        hplanes, hq, hpairs = planes // 2, rows // 4, pairs // 2
        x5 = x.reshape(planes, qs, 2, pairs, feats)
        w1t = jnp.transpose(w1, (0, 1, 2, 4, 3)).reshape(27, ch1, w1.shape[3])
        w2t = jnp.transpose(w2, (0, 1, 2, 4, 3)).reshape(27, ch2, w2.shape[3])
        dma = pltpu.SemaphoreType.DMA
        return pl.pallas_call(
            functools.partial(kernel, n, rows_n),
            out_shape=jax.ShapeDtypeStruct((planes // 4, rows // 4, pairs // 4, 2 * out_ch), BF16),
            in_specs=[pl.BlockSpec(memory_space=pl.ANY), pl.BlockSpec(memory_space=pltpu.VMEM),
                      pl.BlockSpec(memory_space=pl.ANY)],
            out_specs=pl.BlockSpec(memory_space=pltpu.VMEM),
            scratch_shapes=[
                pltpu.VMEM((planes + 1, qs + 1, 2, pairs, feats), BF16),
                pltpu.VMEM((18, n, ch1, feats), BF16),
                pltpu.VMEM((27, n, ch2, mid), BF16),
                pltpu.VMEM((hplanes + 1, hq + 1, 2, hpairs, 2 * mid), BF16),
                pltpu.VMEM((qs * pairs, mid), F32),
                pltpu.VMEM((out_ch // 128, hq * hpairs, 128), F32),
                dma((2,)), dma((1,)), dma((4,)), dma((4,)),
                dma((n // 2,)), dma((n // 2,)), dma((n,)),
                dma((n // 2,)), dma((n // 2,)), dma((n,)),
                dma((3 + hplanes,)), dma((3 + hplanes,)),
            ],
            compiler_params=pltpu.CompilerParams(
                collective_id=0, has_side_effects=True, vmem_limit_bytes=60 * 1024 * 1024),
        )(x5, w1t, w2t)

    return jax.shard_map(
        per_device,
        mesh=mesh,
        in_specs=(
            P("depth", "row", None, None),
            P(None, None, None, None, "depth"),
            P(None, None, None, None, "depth"),
        ),
        out_specs=P("depth", "row", None, None),
        check_vma=False,
    )
```

time: 72.5 us -> 31 us (0.43)
  the two profiles are of different devices: /device:TPU:29 before, /device:TPU:12 now
where the time goes in v1:
time: 31 us; the launch traced here: 30.8 us
  Pallas kernels  29.2 us (94%)
  local copies, waits for them, and re-layouts  1.57 us (5%)
    pallas_call x1, Pallas kernels, per_device(): pl.pallas_call(functools.partial(kernel, n, rows_n), out_shape=jax.ShapeD...  29.2 us
    unnamed x1, local copies, waits for them, and re-layouts  1.57 us

profile of v1, /device:TPU:12, one launch (start us, length us, event | category | flops | bytes accessed | tf_op | source)
XLA Modules:
  0.0 30.8 jit_solution(16747501932526932859)
XLA Ops:
  0.0 29.2 %shard_map.37 = bf16[1,4,32,512]{3,2,1,0:T(8,128)(2,1)} custom-call(bf16[4,8,2,128,128]{4,3,2,1,0:T(8,128)(2,1)} %bitcast.7, bf16[27,16,64]{2,1,0:T(8,128)(2,1)} %bitcast.9, bf16[27,32,128]{2,1,0:T(8,128)(2,1)} %bitcast.8), custom_call_target="tpu_custom_call" | custom-call | tf_op jit(solution)/shard_map/pallas_call | solution.py:252
  29.3 1.6 %copy.5 = bf16[1,4,32,512]{3,2,1,0:T(8,128)(2,1)} copy(bf16[1,4,32,512]{3,2,1,0:T(8,128)(2,1)} %shard_map.37) | data formatting | bytes 262144

commit v2 on v1

--- a/solution.py
+++ b/solution.py
@@ -9,6 +9,8 @@
 
 MESH = pl.DeviceIdType.MESH
 BF16, F32 = jnp.bfloat16, jnp.float32
+CUTS1 = (0, 18)
+CUTS2 = (0, 9, 18, 27)
 
 
 def dot_nt(lhs, rhs):
@@ -29,8 +31,8 @@
 
 
 def kernel(n, rows_n, x_ref, w1_ref, w2_ref, o_ref, ext, g1, g2, hid, tmp, tmp2,
-           x_sem, own_sem, h_send, h_recv, w1_send, w1_fwd, w1_recv,
-           w2_send, w2_fwd, w2_recv, hh_send, hh_recv):
+           x_sem, own_sem, h_send, h_recv, w1_send, w1_recv,
+           w2_send, w2_recv, hh_send, hh_recv):
     d, r = lax.axis_index("depth"), lax.axis_index("row")
     planes, qs = x_ref.shape[0], x_ref.shape[1]
     pairs, feats = x_ref.shape[3], x_ref.shape[4]
@@ -56,20 +58,30 @@
     own_w2.start()
 
     barrier = pltpu.get_barrier_semaphore()
-    for k in range(1, n):
-        pl.semaphore_signal(barrier, inc=1, device_id=(lax.rem(d + k, n), r), device_id_type=MESH)
-
-    @pl.when(has_next_r)
-    def _():
-        pl.semaphore_signal(barrier, inc=1, device_id=(d, r + 1), device_id_type=MESH)
+    relay = n == 8 and rows_n % 2 == 0
+    if relay:
+        chip, core = d // 2, lax.rem(d, 2)
+        x_nbr = chip + 1 - 2 * lax.rem(chip, 2)
+        y_nbr = chip + 2 - 4 * (chip // 2)
+        mate_r = r + 1 - 2 * lax.rem(r, 2)
+        turned = chip == 2
+        u_nbr = jnp.where(turned, x_nbr, y_nbr)
+        v_nbr = jnp.where(turned, y_nbr, x_nbr)
+        g_nbr = 3 - chip
+        mine = core == lax.rem(r, 2)
+        friends = [(partner, r), (2 * x_nbr + core, r), (2 * y_nbr + core, r), (d, mate_r)]
+    else:
+        friends = [(lax.rem(d + k, n), r) for k in range(1, n)]
+    for to in friends:
+        pl.semaphore_signal(barrier, inc=1, device_id=to, device_id_type=MESH)
+
+    @pl.when(has_prev_d)
+    def _():
+        pl.semaphore_signal(barrier, inc=1, device_id=(d - 1, r), device_id_type=MESH)
 
     @pl.when(has_prev_r)
     def _():
         pl.semaphore_signal(barrier, inc=1, device_id=(d, r - 1), device_id_type=MESH)
-
-    @pl.when(has_next_r & has_next_d)
-    def _():
-        pl.semaphore_signal(barrier, inc=1, device_id=(d + 1, r + 1), device_id_type=MESH)
 
     @pl.when(has_prev_r & has_prev_d)
     def _():
@@ -90,9 +102,8 @@
         ext[:, 0, 0] = jnp.zeros((planes + 1, pairs, feats), BF16)
         hid[:, 0, 0] = jnp.zeros((hplanes + 1, hpairs, 2 * mid), BF16)
 
-    expected = (n - 1 + has_next_r.astype(jnp.int32) + has_prev_r.astype(jnp.int32)
-                + (has_next_r & has_next_d).astype(jnp.int32)
-                + (has_prev_r & has_prev_d).astype(jnp.int32))
+    expected = (len(friends) + has_next_d.astype(jnp.int32) + has_next_r.astype(jnp.int32)
+                + (has_next_r & has_next_d).astype(jnp.int32))
     pl.semaphore_wait(barrier, expected)
 
     def remote(src, dst, ssem, rsem, to):
@@ -100,22 +111,90 @@
             src_ref=src, dst_ref=dst, send_sem=ssem, recv_sem=rsem,
             device_id=to, device_id_type=MESH)
 
-    def weight_copy(src, buf, owner, ssem, rsem, to):
-        return remote(src, buf.at[:, owner], ssem, rsem.at[owner], (to, r))
-
-    def same(k):
-        return lax.rem(d + 2 * k, n)
-
-    w1_out = [weight_copy(g1.at[:, d], g1, d, w1_send.at[0], w1_recv, partner)]
-    w2_out = [weight_copy(w2_ref, g2, d, w2_send.at[0], w2_recv, partner)]
-    for k in range(1, n // 2):
-        w1_out.append(weight_copy(g1.at[:, d], g1, d, w1_send.at[k], w1_recv, same(k)))
-        w2_out.append(weight_copy(w2_ref, g2, d, w2_send.at[k], w2_recv, same(k)))
-    w1_on = [weight_copy(g1.at[:, same(k)], g1, same(k), w1_fwd.at[k], w1_recv, partner) for k in range(1, n // 2)]
-    w2_on = [weight_copy(g2.at[:, same(k)], g2, same(k), w2_fwd.at[k], w2_recv, partner) for k in range(1, n // 2)]
-
-    def arrived(buf, rsem, owner):
-        remote(buf.at[:, owner], buf.at[:, owner], rsem.at[owner], rsem.at[owner], (partner, r)).wait_recv()
+    def when_start(cond, copies):
+        @pl.when(cond)
+        def _():
+            for c in copies:
+                c.start()
+
+    def when_recv(cond, copies):
+        @pl.when(cond)
+        def _():
+            for c in copies:
+                c.wait_recv()
+
+    def when_sent(cond, copies):
+        @pl.when(cond)
+        def _():
+            for c in copies:
+                c.wait_send()
+
+    always = n > 0
+    sent = []
+
+    class Gather:
+        def __init__(self, buf, own, ssem, rsem, cuts):
+            self.buf, self.own, self.ssem, self.rsem = buf, own, ssem, rsem
+            self.cuts = list(zip(cuts[:-1], cuts[1:]))
+            self.used = 0
+
+        def copy(self, owner, j, to, own=False):
+            lo, hi = self.cuts[j]
+            place = self.buf.at[lo:hi, owner]
+            c = remote(self.own.at[lo:hi] if own else place, place, self.ssem.at[self.used],
+                       self.rsem.at[owner * len(self.cuts) + j], to)
+            self.used += 1
+            return c
+
+        def send(self, cond, owner, j, to, own=False):
+            c = self.copy(owner, j, to, own)
+            sent.append((cond, c))
+            if cond is always:
+                c.start()
+            else:
+                when_start(cond, [c])
+
+        def wait(self, owner, j):
+            lo, hi = self.cuts[j]
+            place = self.buf.at[lo:hi, owner]
+            sem = self.rsem.at[owner * len(self.cuts) + j]
+            remote(place, place, sem, sem, (partner, r)).wait_recv()
+
+        def send_own(self):
+            for j in range(len(self.cuts)):
+                if relay:
+                    self.send((chip == 3) | mine, d, j, (2 * x_nbr + core, r), True)
+                    self.send((chip != 0) | mine, d, j, (2 * y_nbr + core, r), True)
+                else:
+                    for k in range(1, n // 2):
+                        self.send(always, d, j, (lax.rem(d + 2 * k, n), r), True)
+            for j in range(len(self.cuts)):
+                self.send(always, d, j, (partner, r), True)
+
+        def stage(self, which, j):
+            if not relay:
+                if which == "g":
+                    for k in range(1, n // 2):
+                        self.wait(lax.rem(d + 2 * k, n), j)
+                        self.send(always, lax.rem(d + 2 * k, n), j, (partner, r))
+                return
+            owner = 2 * {"u": u_nbr, "v": v_nbr, "g": g_nbr}[which] + core
+            self.wait(owner, j)
+            if which == "u":
+                self.send(mine & (chip >= 2), owner, j, (2 * jnp.where(turned, y_nbr, x_nbr) + core, r))
+            if which == "v":
+                self.send(mine & ((chip == 1) | (chip == 3)), owner, j, (2 * y_nbr + core, r))
+            if which != "u":
+                self.send(mine, owner, j, (d, mate_r))
+            self.send(always, owner, j, (partner, r))
+
+        def rest(self):
+            for j in range(len(self.cuts)):
+                for k in range(0, n // 2):
+                    self.wait(lax.rem(partner + 2 * k, n), j)
+
+    gather1 = Gather(g1, g1.at[:, d], w1_send, w1_recv, CUTS1)
+    gather2 = Gather(g2, w2_ref, w2_send, w2_recv, CUTS2)
 
     next_d, next_r = lax.rem(d + 1, n), lax.rem(r + 1, rows_n)
     plane_out = [
@@ -125,37 +204,16 @@
     row_out = [remote(x_ref.at[:, qs - 1, 1], ext.at[1:planes + 1, 0, 0], h_send.at[2], h_recv.at[2], (d, next_r))]
     corner_out = [remote(x_ref.at[planes - 1, qs - 1, 1], ext.at[0, 0, 0], h_send.at[3], h_recv.at[3], (next_d, next_r))]
 
-    def when_start(cond, copies):
-        @pl.when(cond)
-        def _():
-            for c in copies:
-                c.start()
-
-    def when_recv(cond, copies):
-        @pl.when(cond)
-        def _():
-            for c in copies:
-                c.wait_recv()
-
-    def when_sent(cond, copies):
-        @pl.when(cond)
-        def _():
-            for c in copies:
-                c.wait_send()
-
-    for c in w1_out:
-        c.start()
+    gather1.send_own()
     when_start(has_next_r, row_out)
+    gather2.send_own()
     when_start(has_next_d, plane_out)
     when_start(has_next_d & has_next_r, corner_out)
-    for c in w2_out:
-        c.start()
-
-    for k in range(1, n // 2):
-        arrived(g1, w1_recv, same(k))
-        w1_on[k - 1].start()
-    for k in range(0, n // 2):
-        arrived(g1, w1_recv, lax.rem(partner + 2 * k, n))
+
+    for which in "uvg":
+        for j in range(len(CUTS1) - 1):
+            gather1.stage(which, j)
+    gather1.rest()
     for c in own_x:
         c.wait()
     when_recv(has_prev_r, row_out)
@@ -196,12 +254,14 @@
             when_start(has_next_d, hplane_out)
             when_start(has_next_d & has_next_r, hcorner_out)
         when_start(has_next_r, [hrow_out[a]])
-
-    for k in range(1, n // 2):
-        arrived(g2, w2_recv, same(k))
-        w2_on[k - 1].start()
-    for k in range(0, n // 2):
-        arrived(g2, w2_recv, lax.rem(partner + 2 * k, n))
+        if a == hplanes - 1:
+            for which in "uv":
+                for j in range(len(CUTS2) - 1):
+                    gather2.stage(which, j)
+
+    for j in range(len(CUTS2) - 1):
+        gather2.stage("g", j)
+    gather2.rest()
     own_w2.wait()
     when_recv(has_prev_r, hrow_out)
     when_recv(has_prev_d, hplane_out)
@@ -229,8 +289,8 @@
                 at = s * out_ch + h * 128
                 o_ref[a, :, :, at:at + 128] = part
 
-    for c in w1_out + w1_on + w2_out + w2_on:
-        c.wait_send()
+    for cond, c in sent:
+        when_sent(cond, [c])
     when_sent(has_next_r, row_out + hrow_out)
     when_sent(has_next_d, plane_out + hplane_out)
     when_sent(has_next_d & has_next_r, corner_out + hcorner_out)
@@ -249,6 +309,7 @@
         w1t = jnp.transpose(w1, (0, 1, 2, 4, 3)).reshape(27, ch1, w1.shape[3])
         w2t = jnp.transpose(w2, (0, 1, 2, 4, 3)).reshape(27, ch2, w2.shape[3])
         dma = pltpu.SemaphoreType.DMA
+        sends = max(n, 11)
         return pl.pallas_call(
             functools.partial(kernel, n, rows_n),
             out_shape=jax.ShapeDtypeStruct((planes // 4, rows // 4, pairs // 4, 2 * out_ch), BF16),
@@ -263,8 +324,8 @@
                 pltpu.VMEM((qs * pairs, mid), F32),
                 pltpu.VMEM((out_ch // 128, hq * hpairs, 128), F32),
                 dma((2,)), dma((1,)), dma((4,)), dma((4,)),
-                dma((n // 2,)), dma((n // 2,)), dma((n,)),
-                dma((n // 2,)), dma((n // 2,)), dma((n,)),
+                dma((sends * (len(CUTS1) - 1),)), dma((n * (len(CUTS1) - 1),)),
+                dma((sends * (len(CUTS2) - 1),)), dma((n * (len(CUTS2) - 1),)),
                 dma((3 + hplanes,)), dma((3 + hplanes,)),
             ],
             compiler_params=pltpu.CompilerParams(

time: 31 us -> 31.8 us (1.026)
  the two profiles are of different devices: /device:TPU:12 before, /device:TPU:0 now
where the time goes in v2:
time: 31.8 us; the launch traced here: 31.6 us
  Pallas kernels  30.1 us (95%)
  local copies, waits for them, and re-layouts  1.57 us (5%)
    pallas_call x1, Pallas kernels, per_device(): pl.pallas_call(functools.partial(kernel, n, rows_n), out_shape=jax.ShapeD...  30.1 us
    unnamed x1, local copies, waits for them, and re-layouts  1.57 us

profile of v2, /device:TPU:0, one launch (start us, length us, event | category | flops | bytes accessed | tf_op | source)
XLA Modules:
  0.0 31.6 jit_solution(3306996005182794522)
XLA Ops:
  0.0 30.1 %shard_map.37 = bf16[1,4,32,512]{3,2,1,0:T(8,128)(2,1)} custom-call(bf16[4,8,2,128,128]{4,3,2,1,0:T(8,128)(2,1)} %bitcast.7, bf16[27,16,64]{2,1,0:T(8,128)(2,1)} %bitcast.9, bf16[27,32,128]{2,1,0:T(8,128)(2,1)} %bitcast.8), custom_call_target="tpu_custom_call" | custom-call | tf_op jit(solution)/shard_map/pallas_call | solution.py:313
  30.1 1.6 %copy.5 = bf16[1,4,32,512]{3,2,1,0:T(8,128)(2,1)} copy(bf16[1,4,32,512]{3,2,1,0:T(8,128)(2,1)} %shard_map.37) | data formatting | bytes 262144

commit v3 on v2

--- a/solution.py
+++ b/solution.py
@@ -69,7 +69,7 @@
         v_nbr = jnp.where(turned, y_nbr, x_nbr)
         g_nbr = 3 - chip
         mine = core == lax.rem(r, 2)
-        friends = [(partner, r), (2 * x_nbr + core, r), (2 * y_nbr + core, r), (d, mate_r)]
+        friends = [(partner, r), (2 * x_nbr + core, r), (2 * y_nbr + core, r), (2 * g_nbr + core, r), (d, mate_r)]
     else:
         friends = [(lax.rem(d + k, n), r) for k in range(1, n)]
     for to in friends:
@@ -133,10 +133,11 @@
     sent = []
 
     class Gather:
-        def __init__(self, buf, own, ssem, rsem, cuts):
+        def __init__(self, buf, own, ssem, rsem, cuts, relay):
             self.buf, self.own, self.ssem, self.rsem = buf, own, ssem, rsem
             self.cuts = list(zip(cuts[:-1], cuts[1:]))
             self.used = 0
+            self.relay = relay
 
         def copy(self, owner, j, to, own=False):
             lo, hi = self.cuts[j]
@@ -162,7 +163,7 @@
 
         def send_own(self):
             for j in range(len(self.cuts)):
-                if relay:
+                if self.relay:
                     self.send((chip == 3) | mine, d, j, (2 * x_nbr + core, r), True)
                     self.send((chip != 0) | mine, d, j, (2 * y_nbr + core, r), True)
                 else:
@@ -172,7 +173,7 @@
                 self.send(always, d, j, (partner, r), True)
 
         def stage(self, which, j):
-            if not relay:
+            if not self.relay:
                 if which == "g":
                     for k in range(1, n // 2):
                         self.wait(lax.rem(d + 2 * k, n), j)
@@ -193,8 +194,8 @@
                 for k in range(0, n // 2):
                     self.wait(lax.rem(partner + 2 * k, n), j)
 
-    gather1 = Gather(g1, g1.at[:, d], w1_send, w1_recv, CUTS1)
-    gather2 = Gather(g2, w2_ref, w2_send, w2_recv, CUTS2)
+    gather1 = Gather(g1, g1.at[:, d], w1_send, w1_recv, CUTS1, False)
+    gather2 = Gather(g2, w2_ref, w2_send, w2_recv, CUTS2, relay)
 
     next_d, next_r = lax.rem(d + 1, n), lax.rem(r + 1, rows_n)
     plane_out = [

time: 31.8 us -> 29.1 us (0.915)
  the two profiles are of different devices: /device:TPU:0 before, /device:TPU:29 now
where the time goes in v3:
time: 29.1 us; the launch traced here: 29 us
  Pallas kernels  27.4 us (94%)
  local copies, waits for them, and re-layouts  1.57 us (5%)
    pallas_call x1, Pallas kernels, per_device(): pl.pallas_call(functools.partial(kernel, n, rows_n), out_shape=jax.ShapeD...  27.4 us
    unnamed x1, local copies, waits for them, and re-layouts  1.57 us

profile of v3, /device:TPU:29, one launch (start us, length us, event | category | flops | bytes accessed | tf_op | source)
XLA Modules:
  0.0 29.0 jit_solution(4816251849002454282)
XLA Ops:
  0.0 27.4 %shard_map.37 = bf16[1,4,32,512]{3,2,1,0:T(8,128)(2,1)} custom-call(bf16[4,8,2,128,128]{4,3,2,1,0:T(8,128)(2,1)} %bitcast.7, bf16[27,16,64]{2,1,0:T(8,128)(2,1)} %bitcast.9, bf16[27,32,128]{2,1,0:T(8,128)(2,1)} %bitcast.8), custom_call_target="tpu_custom_call" | custom-call | tf_op jit(solution)/shard_map/pallas_call | solution.py:314
  27.4 1.6 %copy.5 = bf16[1,4,32,512]{3,2,1,0:T(8,128)(2,1)} copy(bf16[1,4,32,512]{3,2,1,0:T(8,128)(2,1)} %shard_map.37) | data formatting | bytes 262144

commit v4 on v3

--- a/solution.py
+++ b/solution.py
@@ -161,33 +161,45 @@
             sem = self.rsem.at[owner * len(self.cuts) + j]
             remote(place, place, sem, sem, (partner, r)).wait_recv()
 
-        def send_own(self):
+        def send_own(self, part):
             for j in range(len(self.cuts)):
-                if self.relay:
-                    self.send((chip == 3) | mine, d, j, (2 * x_nbr + core, r), True)
-                    self.send((chip != 0) | mine, d, j, (2 * y_nbr + core, r), True)
-                else:
+                if self.relay and part == "v":
+                    self.send(mine & (chip != 3), d, j, (2 * x_nbr + core, r), True)
+                    self.send(mine & (chip == 0), d, j, (2 * y_nbr + core, r), True)
+                if self.relay and part == "u":
+                    self.send(chip != 0, d, j, (2 * y_nbr + core, r), True)
+                    self.send(chip == 3, d, j, (2 * x_nbr + core, r), True)
+                if not self.relay and part == "u":
                     for k in range(1, n // 2):
                         self.send(always, d, j, (lax.rem(d + 2 * k, n), r), True)
-            for j in range(len(self.cuts)):
-                self.send(always, d, j, (partner, r), True)
-
-        def stage(self, which, j):
+            if part == "u":
+                for j in range(len(self.cuts)):
+                    self.send(always, d, j, (partner, r), True)
+
+        def stage(self, which, j, direct):
             if not self.relay:
-                if which == "g":
+                if which == "g" and direct:
                     for k in range(1, n // 2):
                         self.wait(lax.rem(d + 2 * k, n), j)
                         self.send(always, lax.rem(d + 2 * k, n), j, (partner, r))
                 return
             owner = 2 * {"u": u_nbr, "v": v_nbr, "g": g_nbr}[which] + core
-            self.wait(owner, j)
             if which == "u":
+                self.wait(owner, j)
                 self.send(mine & (chip >= 2), owner, j, (2 * jnp.where(turned, y_nbr, x_nbr) + core, r))
-            if which == "v":
-                self.send(mine & ((chip == 1) | (chip == 3)), owner, j, (2 * y_nbr + core, r))
-            if which != "u":
+                self.send(always, owner, j, (partner, r))
+                return
+            here = mine if direct else jnp.logical_not(mine)
+
+            @pl.when(here)
+            def _():
+                self.wait(owner, j)
+
+            if direct:
+                if which == "v":
+                    self.send(mine & ((chip == 1) | (chip == 3)), owner, j, (2 * y_nbr + core, r))
                 self.send(mine, owner, j, (d, mate_r))
-            self.send(always, owner, j, (partner, r))
+            self.send(here, owner, j, (partner, r))
 
         def rest(self):
             for j in range(len(self.cuts)):
@@ -205,16 +217,21 @@
     row_out = [remote(x_ref.at[:, qs - 1, 1], ext.at[1:planes + 1, 0, 0], h_send.at[2], h_recv.at[2], (d, next_r))]
     corner_out = [remote(x_ref.at[planes - 1, qs - 1, 1], ext.at[0, 0, 0], h_send.at[3], h_recv.at[3], (next_d, next_r))]
 
-    gather1.send_own()
+    pieces1, pieces2 = range(len(CUTS1) - 1), range(len(CUTS2) - 1)
+    gather1.send_own("u")
+    gather2.send_own("v")
     when_start(has_next_r, row_out)
-    gather2.send_own()
     when_start(has_next_d, plane_out)
     when_start(has_next_d & has_next_r, corner_out)
-
-    for which in "uvg":
-        for j in range(len(CUTS1) - 1):
-            gather1.stage(which, j)
+    gather2.send_own("u")
+
+    for which, direct in (("u", True), ("v", False), ("g", True)):
+        pass
+    for j in pieces1:
+        gather1.stage("g", j, True)
     gather1.rest()
+    for j in pieces2:
+        gather2.stage("v", j, True)
     for c in own_x:
         c.wait()
     when_recv(has_prev_r, row_out)
@@ -256,12 +273,12 @@
             when_start(has_next_d & has_next_r, hcorner_out)
         when_start(has_next_r, [hrow_out[a]])
         if a == hplanes - 1:
-            for which in "uv":
-                for j in range(len(CUTS2) - 1):
-                    gather2.stage(which, j)
-
-    for j in range(len(CUTS2) - 1):
-        gather2.stage("g", j)
+            for which, direct in (("u", True), ("v", False), ("g", True)):
+                for j in pieces2:
+                    gather2.stage(which, j, direct)
+
+    for j in pieces2:
+        gather2.stage("g", j, False)
     gather2.rest()
     own_w2.wait()
     when_recv(has_prev_r, hrow_out)
@@ -310,7 +327,7 @@
         w1t = jnp.transpose(w1, (0, 1, 2, 4, 3)).reshape(27, ch1, w1.shape[3])
         w2t = jnp.transpose(w2, (0, 1, 2, 4, 3)).reshape(27, ch2, w2.shape[3])
         dma = pltpu.SemaphoreType.DMA
-        sends = max(n, 11)
+        sends = max(n, 14)
         return pl.pallas_call(
             functools.partial(kernel, n, rows_n),
             out_shape=jax.ShapeDtypeStruct((planes // 4, rows // 4, pairs // 4, 2 * out_ch), BF16),

time: 29.1 us -> 28 us (0.962)
  Pallas kernels: 27.4 us -> 26.3 us
    pallas_call x1, Pallas kernels: 27.4 us -> 26.3 us  [per_device(): pl.pallas_call(functools.partial(kernel, n, rows_n), out_shape=jax.ShapeD...]
where the time goes in v4:
time: 28 us; the launch traced here: 27.9 us
  Pallas kernels  26.3 us (94%)
  local copies, waits for them, and re-layouts  1.57 us (6%)
    pallas_call x1, Pallas kernels, per_device(): pl.pallas_call(functools.partial(kernel, n, rows_n), out_shape=jax.ShapeD...  26.3 us
    unnamed x1, local copies, waits for them, and re-layouts  1.57 us

profile of v4, /device:TPU:29, one launch (start us, length us, event | category | flops | bytes accessed | tf_op | source)
XLA Modules:
  0.0 27.9 jit_solution(7633400730633691354)
XLA Ops:
  0.0 26.3 %shard_map.37 = bf16[1,4,32,512]{3,2,1,0:T(8,128)(2,1)} custom-call(bf16[4,8,2,128,128]{4,3,2,1,0:T(8,128)(2,1)} %bitcast.7, bf16[27,16,64]{2,1,0:T(8,128)(2,1)} %bitcast.9, bf16[27,32,128]{2,1,0:T(8,128)(2,1)} %bitcast.8), custom_call_target="tpu_custom_call" | custom-call | tf_op jit(solution)/shard_map/pallas_call | solution.py:331
  26.3 1.6 %copy.5 = bf16[1,4,32,512]{3,2,1,0:T(8,128)(2,1)} copy(bf16[1,4,32,512]{3,2,1,0:T(8,128)(2,1)} %shard_map.37) | data formatting | bytes 262144

commit v5 on v4

--- a/solution.py
+++ b/solution.py
@@ -221,14 +221,14 @@
     gather1.send_own("u")
     gather2.send_own("v")
     when_start(has_next_r, row_out)
-    when_start(has_next_d, plane_out)
-    when_start(has_next_d & has_next_r, corner_out)
     gather2.send_own("u")
 
     for which, direct in (("u", True), ("v", False), ("g", True)):
         pass
     for j in pieces1:
         gather1.stage("g", j, True)
+    when_start(has_next_d, plane_out)
+    when_start(has_next_d & has_next_r, corner_out)
     gather1.rest()
     for j in pieces2:
         gather2.stage("v", j, True)

time: 28 us -> 26.9 us (0.961)
  Pallas kernels: 26.3 us -> 25.2 us
    pallas_call x1, Pallas kernels: 26.3 us -> 25.2 us  [per_device(): pl.pallas_call(functools.partial(kernel, n, rows_n), out_shape=jax.ShapeD...]
where the time goes in v5:
time: 26.9 us; the launch traced here: 26.7 us
  Pallas kernels  25.2 us (94%)
  local copies, waits for them, and re-layouts  1.57 us (6%)
    pallas_call x1, Pallas kernels, per_device(): pl.pallas_call(functools.partial(kernel, n, rows_n), out_shape=jax.ShapeD...  25.2 us
    unnamed x1, local copies, waits for them, and re-layouts  1.57 us

profile of v5, /device:TPU:29, one launch (start us, length us, event | category | flops | bytes accessed | tf_op | source)
XLA Modules:
  0.0 26.7 jit_solution(17012852240012343729)
XLA Ops:
  0.0 25.2 %shard_map.37 = bf16[1,4,32,512]{3,2,1,0:T(8,128)(2,1)} custom-call(bf16[4,8,2,128,128]{4,3,2,1,0:T(8,128)(2,1)} %bitcast.7, bf16[27,16,64]{2,1,0:T(8,128)(2,1)} %bitcast.9, bf16[27,32,128]{2,1,0:T(8,128)(2,1)} %bitcast.8), custom_call_target="tpu_custom_call" | custom-call | tf_op jit(solution)/shard_map/pallas_call | solution.py:331
  25.2 1.6 %copy.5 = bf16[1,4,32,512]{3,2,1,0:T(8,128)(2,1)} copy(bf16[1,4,32,512]{3,2,1,0:T(8,128)(2,1)} %shard_map.37) | data formatting | bytes 262144

commit v6 on v5

--- a/solution.py
+++ b/solution.py
@@ -9,7 +9,7 @@
 
 MESH = pl.DeviceIdType.MESH
 BF16, F32 = jnp.bfloat16, jnp.float32
-CUTS1 = (0, 18)
+CUTS1 = (0, 14)
 CUTS2 = (0, 9, 18, 27)
 
 
@@ -90,7 +90,9 @@
     zero_half = jnp.zeros((w1_ref.shape[1], c1), BF16)
     for ij in range(9):
         g1[ij, d] = jnp.concatenate([w1_ref[3 * ij + 1], w1_ref[3 * ij + 2]], 1)
-        g1[9 + ij, d] = jnp.concatenate([zero_half, w1_ref[3 * ij]], 1)
+    for m in range(5):
+        low = w1_ref[6 * m + 3] if m < 4 else zero_half
+        g1[9 + m, d] = jnp.concatenate([low, w1_ref[6 * m]], 1)
 
     @pl.when(jnp.logical_not(has_prev_d))
     def _():
@@ -236,8 +238,13 @@
         c.wait()
     when_recv(has_prev_r, row_out)
 
+    def third(ij):
+        tile = merged(g1[9 + ij // 2])
+        part = tile[:, c1:] if ij % 2 == 0 else tile[:, :c1]
+        return jnp.concatenate([jnp.zeros_like(part), part], 1)
+
     rhs1 = jnp.concatenate(
-        [jnp.concatenate([merged(g1[ij]), merged(g1[9 + ij])], 0) for ij in range(9)], 1)
+        [jnp.concatenate([merged(g1[ij]), third(ij)], 0) for ij in range(9)], 1)
 
     def first(a):
         wins = []
@@ -336,7 +343,7 @@
             out_specs=pl.BlockSpec(memory_space=pltpu.VMEM),
             scratch_shapes=[
                 pltpu.VMEM((planes + 1, qs + 1, 2, pairs, feats), BF16),
-                pltpu.VMEM((18, n, ch1, feats), BF16),
+                pltpu.VMEM((14, n, ch1, feats), BF16),
                 pltpu.VMEM((27, n, ch2, mid), BF16),
                 pltpu.VMEM((hplanes + 1, hq + 1, 2, hpairs, 2 * mid), BF16),
                 pltpu.VMEM((qs * pairs, mid), F32),

time: 26.9 us -> 26.3 us (0.978)
  Pallas kernels: 25.2 us -> 24.6 us
    pallas_call x1, Pallas kernels: 25.2 us -> 24.6 us  [per_device(): pl.pallas_call(functools.partial(kernel, n, rows_n), out_shape=jax.ShapeD...]
where the time goes in v6:
time: 26.3 us; the launch traced here: 26.1 us
  Pallas kernels  24.6 us (94%)
  local copies, waits for them, and re-layouts  1.57 us (6%)
    pallas_call x1, Pallas kernels, per_device(): pl.pallas_call(functools.partial(kernel, n, rows_n), out_shape=jax.ShapeD...  24.6 us
    unnamed x1, local copies, waits for them, and re-layouts  1.57 us

profile of v6, /device:TPU:29, one launch (start us, length us, event | category | flops | bytes accessed | tf_op | source)
XLA Modules:
  0.0 26.1 jit_solution(16796463527068425027)
XLA Ops:
  0.0 24.6 %shard_map.37 = bf16[1,4,32,512]{3,2,1,0:T(8,128)(2,1)} custom-call(bf16[4,8,2,128,128]{4,3,2,1,0:T(8,128)(2,1)} %bitcast.7, bf16[27,16,64]{2,1,0:T(8,128)(2,1)} %bitcast.9, bf16[27,32,128]{2,1,0:T(8,128)(2,1)} %bitcast.8), custom_call_target="tpu_custom_call" | custom-call | tf_op jit(solution)/shard_map/pallas_call | solution.py:338
  24.6 1.6 %copy.5 = bf16[1,4,32,512]{3,2,1,0:T(8,128)(2,1)} copy(bf16[1,4,32,512]{3,2,1,0:T(8,128)(2,1)} %shard_map.37) | data formatting | bytes 262144
